TPU v7x, 32 devices: a whole 2x2x4 slice. The times are simulated.
32 devices in a mesh: region: 4 (over z), seq: 8 (over y, x, core).
Axes of the slice: x: 2, y: 2, z: 4, core: 2. Of those that a mesh axis runs over, the one named last changes fastest.
Arguments:
- queries: bfloat16 [4096, 1024], P(('region', 'seq')), may hold values from -80 to 80
- keys: bfloat16 [4096, 1024], P(('region', 'seq')), may hold values from -8 to 8
- values: bfloat16 [4096, 1024], P(('region', 'seq')), may hold values from -6 to 6
- out_grad: bfloat16 [4096, 1024], P(('region', 'seq')), may hold values from -6 to 6
- table: int32 [4, 8, 8], P('region'), may hold values from -1 to 23, as said below
- counts: int32 [4, 8], replicated, may hold values from 2 to 128
- sendlist: int32 [4, 2, 8], replicated, may hold values from 0 to 7, as said below
Outputs:
- attended: bfloat16 [4096, 1024], P(('region', 'seq'))
- query_grad: bfloat16 [4096, 1024], P(('region', 'seq'))
- key_grad: bfloat16 [4096, 1024], P(('region', 'seq'))
- value_grad: bfloat16 [4096, 1024], P(('region', 'seq'))
Inputs may be any that keep to these rules, and one draw needn't show every extreme that they name: `table`: entry 0 of a block is the block itself; entries of one block differ; -1 marks padding and only follows live entries; an entry of 8 or more names boundary slot entry - 8 of key_ext. `sendlist`: the 8 blocks of one list differ.
All inputs are finite; a program needn't handle non-finite values.
Results may differ from a plain program's by a relative error of at most 0.035.
Values may be sent and summed in bfloat16 or wider, within the bound.
A program may use at most 128 MiB of HBM per device.

v0:
```python
from functools import partial
import math
import jax
import jax.numpy as jnp
from jax import lax
from jax.sharding import PartitionSpec as P

H = 16
HD = 64
BLK = 128
NBR = 8
BND = 8


def with_halo(cells, sides, width):
    for axis, dim in sides:
        count = lax.axis_size(axis)
        head = lax.slice_in_dim(cells, 0, width, axis=dim)
        tail = lax.slice_in_dim(cells, cells.shape[dim] - width, cells.shape[dim], axis=dim)
        cells = jnp.concatenate(
            [
                lax.ppermute(tail, axis, [(i, (i + 1) % count) for i in range(count)]),
                cells,
                lax.ppermute(head, axis, [((i + 1) % count, i) for i in range(count)]),
            ],
            axis=dim,
        )
    return cells


def attend_group(carry, inputs, key_ext, value_ext, count_ext, scale):
    key_acc, value_acc = carry
    query_grp, grad_grp, table_grp, count_grp, offset_grp = inputs
    group_size, neighbours = table_grp.shape
    heads = query_grp.shape[1]
    piece_len = query_grp.shape[2]
    depth = query_grp.shape[3]
    block_len = key_ext.shape[2]
    safe_ids = jnp.maximum(table_grp, 0)
    key_rows = key_ext[:, safe_ids].reshape(heads, group_size, neighbours * block_len, depth)
    value_rows = value_ext[:, safe_ids].reshape(heads, group_size, neighbours * block_len, depth)
    positions = jnp.arange(block_len, dtype=jnp.int32)
    key_valid = (table_grp >= 0)[:, :, None] & (
        positions[None, None, :] < count_ext[safe_ids][:, :, None]
    )
    key_valid = key_valid.reshape(group_size, neighbours * block_len)
    query_pos = jnp.arange(piece_len, dtype=jnp.int32)
    query_valid = offset_grp[:, None] + query_pos[None, :] < count_grp[:, None]
    scores = (
        jnp.einsum("bhqe,hbke->bhqk", query_grp, key_rows, preferred_element_type=jnp.float32)
        * scale
    )
    scores = jnp.where(key_valid[:, None, None, :], scores, jnp.float32(-1e30))
    peak = jnp.max(scores, axis=-1, keepdims=True)
    expo = jnp.exp(scores - peak)
    prob = (expo / jnp.sum(expo, axis=-1, keepdims=True)).astype(jnp.bfloat16)
    attended = jnp.einsum("bhqk,hbke->bhqe", prob, value_rows, preferred_element_type=jnp.float32)
    attended = jnp.where(query_valid[:, None, :, None], attended, jnp.float32(0.0)).astype(
        jnp.bfloat16
    )
    grad_masked = jnp.where(query_valid[:, None, :, None], grad_grp, jnp.zeros_like(grad_grp))
    dprob = jnp.einsum(
        "bhqe,hbke->bhqk", grad_masked, value_rows, preferred_element_type=jnp.float32
    )
    delta = jnp.sum(grad_masked.astype(jnp.float32) * attended.astype(jnp.float32), axis=-1)[
        ..., None
    ]
    dscore = (prob.astype(jnp.float32) * (dprob - delta)).astype(jnp.bfloat16)
    query_grad = (
        jnp.einsum("bhqk,hbke->bhqe", dscore, key_rows, preferred_element_type=jnp.float32) * scale
    )
    query_grad = query_grad.astype(jnp.bfloat16)
    key_part = (
        jnp.einsum("bhqk,bhqe->hbke", dscore, query_grp, preferred_element_type=jnp.float32) * scale
    )
    value_part = jnp.einsum(
        "bhqk,bhqe->hbke", prob, grad_masked, preferred_element_type=jnp.float32
    )
    flat_ids = safe_ids.reshape(-1)
    key_acc = key_acc.at[:, flat_ids].add(
        key_part.reshape(heads, group_size * neighbours, block_len, depth)
    )
    value_acc = value_acc.at[:, flat_ids].add(
        value_part.reshape(heads, group_size * neighbours, block_len, depth)
    )
    return ((key_acc, value_acc), (attended, query_grad))


def body(queries, keys, values, out_grad, table, counts, sendlist):
    seq_count = lax.axis_size("seq")
    region_count = lax.axis_size("region")
    galaxies, width = queries.shape
    pair_count = seq_count // 2
    pair_heads = 2 * H // seq_count
    pair_width = pair_heads * HD
    half_rows = galaxies // 2
    region_rows = seq_count * galaxies
    block_total = region_rows // BLK
    parity = lax.axis_index("seq") % 2
    region_now = lax.axis_index("region")

    def half_slots(matrix):
        return (
            matrix.reshape(2, half_rows, pair_count, pair_width)
            .transpose(2, 0, 1, 3)
            .reshape(seq_count, half_rows, pair_width)
        )

    query_heads, grad_heads = (
        lax.all_to_all(half_slots(queries), "seq", split_axis=0, concat_axis=1, tiled=True),
        lax.all_to_all(half_slots(out_grad), "seq", split_axis=0, concat_axis=1, tiled=True),
    )

    def all_slots(matrix):
        grouped = matrix.reshape(galaxies, pair_count, pair_width).transpose(1, 0, 2)
        return jnp.repeat(grouped, 2, axis=0)

    key_heads, value_heads = (
        lax.all_to_all(all_slots(keys), "seq", split_axis=0, concat_axis=1, tiled=True),
        lax.all_to_all(all_slots(values), "seq", split_axis=0, concat_axis=1, tiled=True),
    )
    paired = jnp.stack([key_heads[0], value_heads[0]])
    head_first = paired.reshape(2, region_rows, pair_heads, HD).transpose(0, 2, 1, 3)
    head_blocks = head_first.reshape(2, pair_heads, block_total, BLK, HD)
    my_lists = sendlist[region_now]
    prev_ids = my_lists[0]
    next_ids = my_lists[1]
    rim_rows = BND * BLK
    packed_rim = rim_rows // 2
    outgoing = jnp.concatenate(
        [head_blocks[:, :, prev_ids], head_blocks[:, :, next_ids]], axis=2
    ).reshape(2, pair_heads, rim_rows, 2 * HD)
    widened = with_halo(outgoing, (("region", 2),), packed_rim)
    from_left = widened[:, :, :packed_rim].reshape(2, pair_heads, rim_rows, HD)
    from_right = widened[:, :, -packed_rim:].reshape(2, pair_heads, rim_rows, HD)
    slots = block_total + 2 * BND
    extended = jnp.concatenate([head_first, from_left, from_right], axis=2).reshape(
        2, pair_heads, slots, BLK, HD
    )
    left_region = (region_now + region_count - 1) % region_count
    right_region = (region_now + 1) % region_count
    count_ext = jnp.concatenate(
        [
            counts[region_now],
            counts[left_region][sendlist[left_region, 1]],
            counts[right_region][sendlist[right_region, 0]],
        ]
    )
    piece_rows = min(BLK, half_rows)
    per_source = half_rows // piece_rows
    piece_starts = (
        jnp.arange(seq_count, dtype=jnp.int32)[:, None] * galaxies
        + parity * half_rows
        + jnp.arange(per_source, dtype=jnp.int32)[None, :] * piece_rows
    ).reshape(-1)
    piece_blocks = piece_starts // BLK
    piece_offsets = piece_starts % BLK
    my_table = table[0][piece_blocks]
    my_counts = counts[region_now][piece_blocks]
    piece_total = seq_count * per_source
    group_width = 8
    groups = piece_total // group_width

    def scan_layout(matrix):
        return matrix.reshape(groups, group_width, piece_rows, pair_heads, HD).transpose(
            0, 1, 3, 2, 4
        )

    stepper = partial(
        attend_group,
        key_ext=extended[0],
        value_ext=extended[1],
        count_ext=count_ext,
        scale=1.0 / math.sqrt(HD),
    )
    start = (
        jnp.zeros((pair_heads, slots, BLK, HD), jnp.float32),
        jnp.zeros((pair_heads, slots, BLK, HD), jnp.float32),
    )
    carried, outputs = lax.scan(
        stepper,
        start,
        (
            scan_layout(query_heads),
            scan_layout(grad_heads),
            my_table.reshape(groups, group_width, NBR),
            my_counts.reshape(groups, group_width),
            piece_offsets.reshape(groups, group_width),
        ),
    )
    accum = jnp.stack([carried[0], carried[1]]).reshape(2, pair_heads, slots * BLK, HD)
    inner = accum[:, :, :region_rows].reshape(2, pair_heads, block_total, BLK, HD)
    rim_out = accum[:, :, region_rows:].reshape(2, pair_heads, rim_rows, 2 * HD)
    returned = with_halo(rim_out, (("region", 2),), packed_rim)
    back_left = returned[:, :, :packed_rim].reshape(2, pair_heads, BND, BLK, HD)
    back_right = returned[:, :, -packed_rim:].reshape(2, pair_heads, BND, BLK, HD)
    inner = inner.at[:, :, prev_ids].add(back_left)
    inner = inner.at[:, :, next_ids].add(back_right)
    inner = (
        inner.reshape(2, pair_heads, region_rows, HD)
        .transpose(0, 2, 1, 3)
        .reshape(2, region_rows, pair_width)
    )
    spread = lax.all_to_all(
        inner.reshape(2, seq_count, galaxies, pair_width),
        "seq",
        split_axis=1,
        concat_axis=1,
        tiled=True,
    )
    summed = spread.reshape(2, pair_count, 2, galaxies, pair_width).sum(axis=2)
    grads = summed.transpose(0, 2, 1, 3).reshape(2, galaxies, width)
    attended_heads = outputs[0].transpose(0, 1, 3, 2, 4).reshape(seq_count, half_rows, pair_width)
    qgrad_heads = outputs[1].transpose(0, 1, 3, 2, 4).reshape(seq_count, half_rows, pair_width)
    attended_back, qgrad_back = (
        lax.all_to_all(attended_heads, "seq", split_axis=0, concat_axis=0, tiled=True),
        lax.all_to_all(qgrad_heads, "seq", split_axis=0, concat_axis=0, tiled=True),
    )

    def owner_rows(received):
        return (
            received.reshape(pair_count, 2, half_rows, pair_width)
            .transpose(1, 2, 0, 3)
            .reshape(galaxies, width)
        )

    grads = grads.astype(jnp.bfloat16)
    return (owner_rows(attended_back), owner_rows(qgrad_back), grads[0], grads[1])


def solution(mesh):
    return jax.shard_map(
        body,
        mesh=mesh,
        in_specs=(
            P(("region", "seq"), None),
            P(("region", "seq"), None),
            P(("region", "seq"), None),
            P(("region", "seq"), None),
            P("region", None, None),
            P(),
            P(),
        ),
        out_specs=(
            P(("region", "seq"), None),
            P(("region", "seq"), None),
            P(("region", "seq"), None),
            P(("region", "seq"), None),
        ),
        check_vma=False,
    )
```

profile of v0, /device:TPU:0, one launch (start us, length us, event | category | flops | bytes accessed | tf_op | source)
XLA Modules:
  0.0 426.3 jit_solution(13458127873232549518)
XLA Ops:
  0.7 1.2 reshape.423
  3.0 5.2 %all-to-all-start.1 = ((bf16[8,128,256]{1,2,0:T(8,128)(2,1)}), bf16[8,128,256]{1,2,0:T(8,128)(2,1)S(1)}, u32[]{:S(2)}, u32[]{:S(2)}) async-start(bf16[8,128,256]{1,2,0:T(8,128)(2,1)} %bitcast.15), calls=%async_computation.1 | async-start | bytes 1048576 | tf_op jit(solution)/shard_map/all_to_all | solution.py:120
  11.1 6.8 %all-to-all-done.1 = bf16[8,128,256]{1,2,0:T(8,128)(2,1)S(1)} async-done(((bf16[8,128,256]{1,2,0:T(8,128)(2,1)}), bf16[8,128,256]{1,2,0:T(8,128)(2,1)S(1)}, u32[]{:S(2)}, u32[]{:S(2)}) %all-to-all-start.1) | async-done | bytes 524320 | tf_op jit(solution)/shard_map/all_to_all | solution.py:120
  18.7 3.5 all-to-all-start
  25.1 6.8 %all-to-all-done = bf16[8,128,256]{1,2,0:T(8,128)(2,1)S(1)} async-done(((bf16[8,128,256]{1,2,0:T(8,128)(2,1)}), bf16[8,128,256]{1,2,0:T(8,128)(2,1)S(1)}, u32[]{:S(2)}, u32[]{:S(2)}) %all-to-all-start) | async-done | bytes 524320 | tf_op jit(solution)/shard_map/all_to_all | solution.py:119
  31.9 3.4 all-to-all-start.4
  38.8 1.5 pad_maximum_fusion.1
  40.4 4.8 %copy.175 = bf16[2,4,16,128,64]{4,3,2,1,0:T(8,128)(2,1)} copy(bf16[2,4,16,128,64]{3,4,1,0,2:T(8,128)(2,1)} %pad_maximum_fusion.1) | data formatting | bytes 4194304 | tf_op jit(solution)/shard_map/concatenate | solution.py:130
  45.2 5.0 %reshape.426 = bf16[2,4,1024,128]{3,2,1,0:T(8,128)(2,1)S(1)} reshape(bf16[2,4,16,128,64]{4,3,2,1,0:T(8,128)(2,1)} %copy.175) | data formatting | bytes 4194304 | tf_op jit(solution)/shard_map/reshape | solution.py:132
  50.2 1.5 fusion.66
  51.7 3.6 collective-permute-start.1
  59.3 4.3 %all-to-all-start.2 = ((bf16[8,64,256]{2,1,0:T(8,128)(2,1)}), bf16[8,64,256]{2,1,0:T(8,128)(2,1)S(1)}, u32[]{:S(2)}, u32[]{:S(2)}) async-start(bf16[8,64,256]{2,1,0:T(8,128)(2,1)} %bitcast.26), calls=%async_computation.2 | async-start | bytes 524288 | tf_op jit(solution)/shard_map/all_to_all | solution.py:110
  65.9 4.6 %all-to-all-done.2 = bf16[8,64,256]{2,1,0:T(8,128)(2,1)S(1)} async-done(((bf16[8,64,256]{2,1,0:T(8,128)(2,1)}), bf16[8,64,256]{2,1,0:T(8,128)(2,1)S(1)}, u32[]{:S(2)}, u32[]{:S(2)}) %all-to-all-start.2) | async-done | bytes 262176 | tf_op jit(solution)/shard_map/all_to_all | solution.py:110
  71.6 7.6 %collective-permute-done.1 = bf16[2,4,512,128]{3,2,1,0:T(8,128)(2,1)S(1)} collective-permute-done((bf16[2,4,512,128]{3,2,1,0:T(8,128)(2,1)}, bf16[2,4,512,128]{3,2,1,0:T(8,128)(2,1)S(1)}, u32[]{:S(2)}, u32[]{:S(2)}) %collective-permute-start.1) | collective-permute-done | bytes 1048608 | tf_op jit(solution)/shard_map/ppermute | solution.py:24
  80.1 1.6 copy.177
  81.7 20.3 %collective-permute-done = bf16[2,4,512,128]{3,2,1,0:T(8,128)(2,1)} collective-permute-done((bf16[2,4,512,128]{3,2,1,0:T(8,128)(2,1)}, bf16[2,4,512,128]{3,2,1,0:T(8,128)(2,1)}, u32[]{:S(2)}, u32[]{:S(2)}) %collective-permute-start) | collective-permute-done | bytes 1048608 | tf_op jit(solution)/shard_map/ppermute | solution.py:22
  102.0 2.7 reshape.427
  104.7 1.6 copy.176
  106.4 1.7 pad_maximum_fusion
  109.0 3.1 gather_fusion.7
  112.8 3.0 gather_fusion.8
  115.9 6.7 %fusion.11 = f32[8,4,1024,64]{2,3,1,0:T(8,128)} fusion(bf16[8,8,4,8,8,128]{5,4,3,2,1,0:T(8,128)(2,1)} %bitcast.216, bf16[1,8,64,4,64]{4,3,2,1,0:T(4,128)(2,1)S(1)} %copy-done.4), kind=kOutput, calls=%fused_computation.27 | convolution fusion | flops 268435456 | bytes 12845056 | tf_op jit(solution)/shard_map/while/body/eval_jaxpr/bhqe,hbke->bhqk/dot_general | solution.py:50
  122.5 8.4 %fusion.68 = (f32[8,4,64]{2,1,0:T(4,128)S(1)}, f32[8,4,64,1024]{3,2,1,0:T(8,128)S(1)}) fusion(f32[8,4,1024,64]{2,3,1,0:T(8,128)} %fusion.11, pred[8,1024]{1,0:T(8,128)(4,1)S(1)} %fusion.50), kind=kOutput, calls=%fused_computation.114 | output fusion | flops 12583935 | bytes 16793600 | tf_op jit(solution)/shard_map/while/body/eval_jaxpr/sub | solution.py:55
  133.3 2.0 multiply_reduce_fusion
  135.3 4.5 %fusion.13 = f32[4,8,1024,64]{2,3,1,0:T(8,128)} fusion(bf16[8,4,64,1024]{3,2,1,0:T(8,128)(2,1)S(1)} %divide_convert_fusion, bf16[8,4,64,64]{2,3,1,0:T(8,128)(2,1)S(1)} %get-tuple-element.35), kind=kOutput, calls=%fused_computation.29 | convolution fusion | flops 268435456 | bytes 12845056 | tf_op jit(solution)/shard_map/while/body/eval_jaxpr/bhqk,bhqe->hbke/dot_general | solution.py:76
  139.8 1.9 multiply_convert_fusion
  141.6 1.9 copy-done.3
  143.6 1.3 broadcast_multiply_fusion
  144.9 8.1 %copy.197 = f32[4,8,1024,64]{2,1,3,0:T(8,128)} copy(f32[4,8,1024,64]{2,3,1,0:T(8,128)S(1)} %broadcast_multiply_fusion) | data formatting | bytes 16777216 | tf_op jit(solution)/shard_map/while/body/eval_jaxpr/mul | solution.py:74
  153.0 9.6 %reshape.524 = f32[4,64,128,64]{2,1,3,0:T(8,128)} reshape(f32[4,8,1024,64]{2,1,3,0:T(8,128)} %copy.197) | data formatting | bytes 16777216 | tf_op jit(solution)/shard_map/while/body/eval_jaxpr/reshape | solution.py:81
  162.6 11.5 %copy.198 = f32[64,4,128,64]{2,3,1,0:T(8,128)} copy(f32[64,4,128,64]{2,0,3,1:T(8,128)} %bitcast.220) | data formatting | bytes 16777216 | tf_op jit(solution)/shard_map/while/body/eval_jaxpr/reshape | solution.py:81
  174.5 13.4 %scatter_fusion = f32[4,24,128,64]{2,3,1,0:T(8,128)S(1)} fusion(f32[4,24,128,64]{2,3,1,0:T(8,128)S(1)} %broadcast.273.clone, s32[64]{0:T(128)S(1)} %reshape.485, f32[64,4,128,64]{2,3,1,0:T(8,128)} %copy.198), kind=kCustom, calls=%fused_computation.9 | custom fusion | flops 2097152 | bytes 25166080 | tf_op jit(solution)/shard_map/while/body/eval_jaxpr/scatter-add | solution.py:80
  187.8 3.5 copy.199
  191.4 3.0 stack.19
  194.4 1.9 constant_dynamic-update-slice_fusion.1
  196.2 11.5 %copy.202 = f32[4,8,1024,64]{2,1,3,0:T(8,128)} copy(f32[4,8,1024,64]{2,3,1,0:T(8,128)} %fusion.13) | data formatting | bytes 16777216 | tf_op jit(solution)/shard_map/while/body/eval_jaxpr/bhqk,bhqe->hbke/dot_general | solution.py:76
  207.7 9.3 %reshape.532 = f32[4,64,128,64]{2,1,3,0:T(8,128)} reshape(f32[4,8,1024,64]{2,1,3,0:T(8,128)} %copy.202) | data formatting | bytes 16777216 | tf_op jit(solution)/shard_map/while/body/eval_jaxpr/reshape | solution.py:84
  217.0 11.5 %copy.203 = f32[64,4,128,64]{2,3,1,0:T(8,128)} copy(f32[64,4,128,64]{2,0,3,1:T(8,128)} %bitcast.221) | data formatting | bytes 16777216 | tf_op jit(solution)/shard_map/while/body/eval_jaxpr/reshape | solution.py:84
  228.9 13.6 %scatter_fusion.1 = f32[4,24,128,64]{2,3,1,0:T(8,128)S(1)} fusion(f32[4,24,128,64]{2,3,1,0:T(8,128)S(1)} %broadcast.273.clone.1, s32[64]{0:T(128)S(1)} %reshape.485, f32[64,4,128,64]{2,3,1,0:T(8,128)} %copy.203), kind=kCustom, calls=%fused_computation.10 | custom fusion | flops 2097152 | bytes 25166080 | tf_op jit(solution)/shard_map/while/body/eval_jaxpr/scatter-add | solution.py:83
  242.4 3.5 copy.204
  245.9 2.8 stack.20
  248.7 1.9 constant_dynamic-update-slice_fusion
  250.6 4.6 %slice.77 = f32[2,4,2048,64]{2,3,1,0:T(8,128)} slice(f32[2,4,3072,64]{2,3,1,0:T(8,128)} %constant_dynamic-update-slice_fusion), slice={[0:2], [0:4], [1024:3072], [0:64]} | slice | bytes 8388608 | tf_op jit(solution)/shard_map/slice | solution.py:193
  255.3 6.9 %copy.205 = f32[2,4,2048,64]{3,2,1,0:T(8,128)} copy(f32[2,4,2048,64]{2,3,1,0:T(8,128)} %slice.77) | data formatting | bytes 8388608 | tf_op jit(solution)/shard_map/slice | solution.py:193
  262.2 7.2 %reshape.446 = f32[2,4,1024,128]{3,2,1,0:T(8,128)} reshape(f32[2,4,2048,64]{3,2,1,0:T(8,128)} %copy.205) | data formatting | bytes 8388608 | tf_op jit(solution)/shard_map/reshape | solution.py:193
  269.4 4.8 %fusion.64 = (f32[2,4,512,128]{3,2,1,0:T(8,128)}, f32[2,4,512,128]{3,2,1,0:T(8,128)}) fusion(f32[2,4,1024,128]{3,2,1,0:T(8,128)} %reshape.446), kind=kLoop, calls=%fused_computation.110 | loop fusion | bytes 8388608 | tf_op jit(solution)/shard_map/slice | solution.py:18
  274.2 1.4 collective-permute-start.2
  275.6 2.5 collective-permute-start.3
  279.0 4.1 all-to-all-start.3
  283.1 4.7 %fusion.40 = bf16[1,8,64,4,64]{4,2,3,1,0:T(8,128)(2,1)S(1)} fusion(bf16[8,4,64,1024]{3,2,1,0:T(8,128)(2,1)} %copy-done.3, bf16[8,8,4,8,8,128]{5,4,3,2,1,0:T(8,128)(2,1)} %bitcast.217), kind=kOutput, calls=%fused_computation.51 | convolution fusion | flops 268697600 | bytes 8650752 | tf_op jit(solution)/shard_map/while/body/eval_jaxpr/bhqk,hbke->bhqe/dot_general | solution.py:70
  289.3 1.9 copy_bitcast_fusion.1
  291.1 33.7 %collective-permute-done.2 = f32[2,4,512,128]{3,2,1,0:T(8,128)} collective-permute-done((f32[2,4,512,128]{3,2,1,0:T(8,128)}, f32[2,4,512,128]{3,2,1,0:T(8,128)}, u32[]{:S(2)}, u32[]{:S(2)}) %collective-permute-start.2) | collective-permute-done | bytes 2097184 | tf_op jit(solution)/shard_map/ppermute | solution.py:22
  324.8 4.4 %reshape.540 = f32[2,4,8,128,64]{4,3,2,1,0:T(8,128)} reshape(f32[2,4,512,128]{3,2,1,0:T(8,128)} %collective-permute-done.2) | data formatting | bytes 4194304 | tf_op jit(solution)/shard_map/reshape | solution.py:195
  329.2 3.8 copy.207
  333.0 34.6 %collective-permute-done.3 = f32[2,4,512,128]{3,2,1,0:T(8,128)} collective-permute-done((f32[2,4,512,128]{3,2,1,0:T(8,128)}, f32[2,4,512,128]{3,2,1,0:T(8,128)}, u32[]{:S(2)}, u32[]{:S(2)}) %collective-permute-start.3) | collective-permute-done | bytes 2097184 | tf_op jit(solution)/shard_map/ppermute | solution.py:24
  367.6 4.4 %reshape.548 = f32[2,4,8,128,64]{4,3,2,1,0:T(8,128)} reshape(f32[2,4,512,128]{3,2,1,0:T(8,128)} %collective-permute-done.3) | data formatting | bytes 4194304 | tf_op jit(solution)/shard_map/reshape | solution.py:196
  372.0 3.8 copy.208
  375.8 3.5 scatter_fusion.2
  379.3 3.5 scatter_fusion.3
  382.8 3.6 all-to-all-start.5
  387.2 1.7 copy.210
  388.9 4.4 %all-to-all-done.5 = bf16[8,64,256]{2,1,0:T(8,128)(2,1)S(1)} async-done(((bf16[8,64,256]{2,1,0:T(8,128)(2,1)}), bf16[8,64,256]{2,1,0:T(8,128)(2,1)S(1)}, u32[]{:S(2)}, u32[]{:S(2)}) %all-to-all-start.5) | async-done | bytes 262176 | tf_op jit(solution)/shard_map/all_to_all | solution.py:217
  393.3 3.6 all-to-all-start.6
  398.8 24.6 %all-to-all-done.6 = f32[2,8,128,256]{2,3,0,1:T(8,128)S(1)} async-done(((f32[2,8,128,256]{2,3,0,1:T(8,128)}), f32[2,8,128,256]{2,3,0,1:T(8,128)S(1)}, u32[]{:S(2)}, u32[]{:S(2)}) %all-to-all-start.6) | async-done | bytes 2097184 | tf_op jit(solution)/shard_map/all_to_all | solution.py:204
  (97 shorter events, 31.5 us)
Async XLA Ops:
  0.6 23.2 %copy-start = (s32[1,8,8]{2,1,0:T(8,128)S(1)}, s32[1,8,8]{2,1,0:T(8,128)}, u32[]{:S(2)}) copy-start(s32[1,8,8]{2,1,0:T(8,128)} %param.11) | copy-start | bytes 772
  0.6 22.3 %copy-start.8 = (bf16[128,1024]{1,0:T(8,128)(2,1)S(1)}, bf16[128,1024]{1,0:T(8,128)(2,1)}, u32[]{:S(2)}) copy-start(bf16[128,1024]{1,0:T(8,128)(2,1)} %param.10) | copy-start | bytes 786436
  3.0 14.9 %all-to-all-start.1 = ((bf16[8,128,256]{1,2,0:T(8,128)(2,1)}), bf16[8,128,256]{1,2,0:T(8,128)(2,1)S(1)}, u32[]{:S(2)}, u32[]{:S(2)}) async-start(bf16[8,128,256]{1,2,0:T(8,128)(2,1)} %bitcast.15), calls=%async_computation.1 | async-start | bytes 1048576 | tf_op jit(solution)/shard_map/all_to_all | solution.py:120
  11.1 13.4 %copy-start.9 = (s32[8]{0:T(128)}, s32[8]{0:T(128)S(1)}, u32[]{:S(2)}) copy-start(s32[8]{0:T(128)S(1)} %get-tuple-element.65) | copy-start | bytes 100
  11.1 13.4 %copy-start.11 = (s32[8]{0:T(128)}, s32[8]{0:T(128)S(1)}, u32[]{:S(2)}) copy-start(s32[8]{0:T(128)S(1)} %get-tuple-element.64) | copy-start | bytes 100
  18.7 13.1 %all-to-all-start = ((bf16[8,128,256]{1,2,0:T(8,128)(2,1)}), bf16[8,128,256]{1,2,0:T(8,128)(2,1)S(1)}, u32[]{:S(2)}, u32[]{:S(2)}) async-start(bf16[8,128,256]{1,2,0:T(8,128)(2,1)} %bitcast.13), calls=%async_computation | async-start | bytes 1048576 | tf_op jit(solution)/shard_map/all_to_all | solution.py:119
  31.9 27.4 %all-to-all-start.4 = ((bf16[8,64,256]{2,1,0:T(8,128)(2,1)}), bf16[8,64,256]{2,1,0:T(8,128)(2,1)S(1)}, u32[]{:S(2)}, u32[]{:S(2)}) async-start(bf16[8,64,256]{2,1,0:T(8,128)(2,1)} %bitcast.38), calls=%async_computation.4 | async-start | bytes 524288 | tf_op jit(solution)/shard_map/all_to_all | solution.py:111
  51.7 27.5 %collective-permute-start.1 = (bf16[2,4,512,128]{3,2,1,0:T(8,128)(2,1)}, bf16[2,4,512,128]{3,2,1,0:T(8,128)(2,1)S(1)}, u32[]{:S(2)}, u32[]{:S(2)}) collective-permute-start(bf16[2,4,512,128]{3,2,1,0:T(8,128)(2,1)} %get-tuple-element.54), channel_id=1, source_target_pairs={{8,0},{16,8},{24,16},{0,24},{9,1},{17,9},{25,17},{1,25},{10,2},{18... | collective-permute-start | bytes 3145736 | tf_op jit(solution)/shard_map/ppermute | solution.py:24
  55.3 46.7 %collective-permute-start = (bf16[2,4,512,128]{3,2,1,0:T(8,128)(2,1)}, bf16[2,4,512,128]{3,2,1,0:T(8,128)(2,1)}, u32[]{:S(2)}, u32[]{:S(2)}) collective-permute-start(bf16[2,4,512,128]{3,2,1,0:T(8,128)(2,1)} %get-tuple-element.53), channel_id=1, source_target_pairs={{0,8},{8,16},{16,24},{24,0},{1,9},{9,17},{17,25},{25,1},{2,10},{10... | collective-permute-start | bytes 3145736 | tf_op jit(solution)/shard_map/ppermute | solution.py:22
  59.3 11.2 %all-to-all-start.2 = ((bf16[8,64,256]{2,1,0:T(8,128)(2,1)}), bf16[8,64,256]{2,1,0:T(8,128)(2,1)S(1)}, u32[]{:S(2)}, u32[]{:S(2)}) async-start(bf16[8,64,256]{2,1,0:T(8,128)(2,1)} %bitcast.26), calls=%async_computation.2 | async-start | bytes 524288 | tf_op jit(solution)/shard_map/all_to_all | solution.py:110
  80.1 26.3 %copy-start.5 = (bf16[2,4,1024,64]{2,3,1,0:T(8,128)(2,1)S(1)}, bf16[2,4,1024,64]{2,3,1,0:T(8,128)(2,1)}, u32[]{:S(2)}) copy-start(bf16[2,4,1024,64]{2,3,1,0:T(8,128)(2,1)} %get-tuple-element.55) | copy-start | bytes 3145732
  112.8 3.1 copy-start.4
  131.0 2.2 copy-start.2
  131.0 2.3 copy-start.7
  141.6 1.9 copy-start.3
  269.4 8.6 %copy-start.6 = (bf16[8,4,64,64]{2,3,1,0:T(8,128)(2,1)S(1)}, bf16[8,4,64,64]{2,3,1,0:T(8,128)(2,1)}, u32[]{:S(2)}) copy-start(bf16[8,4,64,64]{2,3,1,0:T(8,128)(2,1)} %get-tuple-element.68) | copy-start | bytes 786436
  274.2 50.6 %collective-permute-start.2 = (f32[2,4,512,128]{3,2,1,0:T(8,128)}, f32[2,4,512,128]{3,2,1,0:T(8,128)}, u32[]{:S(2)}, u32[]{:S(2)}) collective-permute-start(f32[2,4,512,128]{3,2,1,0:T(8,128)} %get-tuple-element.37), channel_id=1, source_target_pairs={{0,8},{8,16},{16,24},{24,0},{1,9},{9,17},{17,25},{25,1},{2,10},{10... | collective-permute-start | bytes 6291464 | tf_op jit(solution)/shard_map/ppermute | solution.py:22
  275.6 92.1 %collective-permute-start.3 = (f32[2,4,512,128]{3,2,1,0:T(8,128)}, f32[2,4,512,128]{3,2,1,0:T(8,128)}, u32[]{:S(2)}, u32[]{:S(2)}) collective-permute-start(f32[2,4,512,128]{3,2,1,0:T(8,128)} %get-tuple-element.36), channel_id=1, source_target_pairs={{8,0},{16,8},{24,16},{0,24},{9,1},{17,9},{25,17},{1,25},{10,2},{18... | collective-permute-start | bytes 6291464 | tf_op jit(solution)/shard_map/ppermute | solution.py:24
  279.0 103.9 %all-to-all-start.3 = ((bf16[8,64,256]{2,1,0:T(8,128)(2,1)}), bf16[8,64,256]{2,1,0:T(8,128)(2,1)S(1)}, u32[]{:S(2)}, u32[]{:S(2)}) async-start(bf16[8,64,256]{2,1,0:T(8,128)(2,1)} %copy.186), calls=%async_computation.3 | async-start | bytes 524288 | tf_op jit(solution)/shard_map/all_to_all | solution.py:216
  372.0 3.8 copy-start.12
  375.8 3.5 copy-start.10
  382.8 10.5 %all-to-all-start.5 = ((bf16[8,64,256]{2,1,0:T(8,128)(2,1)}), bf16[8,64,256]{2,1,0:T(8,128)(2,1)S(1)}, u32[]{:S(2)}, u32[]{:S(2)}) async-start(bf16[8,64,256]{2,1,0:T(8,128)(2,1)} %reshape.440), calls=%async_computation.5 | async-start | bytes 524288 | tf_op jit(solution)/shard_map/all_to_all | solution.py:217
  393.3 30.2 %all-to-all-start.6 = ((f32[2,8,128,256]{2,3,0,1:T(8,128)}), f32[2,8,128,256]{2,3,0,1:T(8,128)S(1)}, u32[]{:S(2)}, u32[]{:S(2)}) async-start(f32[2,8,128,256]{2,3,0,1:T(8,128)} %copy.210), calls=%async_computation.6 | async-start | bytes 4194304 | tf_op jit(solution)/shard_map/all_to_all | solution.py:204
  397.1 28.8 %copy-start.1 = (s32[1,8,8]{2,1,0:T(8,128)S(1)}, s32[1,8,8]{2,1,0:T(8,128)}, u32[]{:S(2)}) copy-start(s32[1,8,8]{2,1,0:T(8,128)} %param.11) | copy-start | bytes 772
where the time goes:
time: 434 us; the launch traced here: 426 us
  local copies, waits for them, and re-layouts  176 us (41%)
  waiting for transfers between devices  144 us (33%)
  other arithmetic  48.8 us (11%)
  starting transfers between devices  35.2 us (8%)
  matrix products  21 us (5%)
    ppermute x2, waiting for transfers between devices, with_halo(): lax.ppermute(tail, axis, [(i, (i + 1) % count) for i in range(count)])  54 us
    ppermute x2, waiting for transfers between devices, with_halo(): lax.ppermute(head, axis, [((i + 1) % count, i) for i in range(count)])  42.2 us
    all_to_all x1, waiting for transfers between devices, body(): lax.all_to_all(inner.reshape(2, seq_count, galaxies, pair_width), 'seq',...  24.6 us
    reshape x2, local copies, waits for them, and re-layouts, attend_group(): key_part.reshape(heads, group_size * neighbours, block_len, depth)  21.1 us
    reshape x2, local copies, waits for them, and re-layouts, attend_group(): value_part.reshape(heads, group_size * neighbours, block_len, depth)  20.8 us
    scatter-add x1, other arithmetic, attend_group(): value_acc.at[:, flat_ids]  13.6 us
    scatter-add x1, other arithmetic, attend_group(): key_acc.at[:, flat_ids]  13.4 us
    slice x2, local copies, waits for them, and re-layouts, body(): rim_out = accum[:, :, region_rows:].reshape(2, pair_heads, rim_rows, 2 * HD)  11.6 us
  transfers between devices with their start and end apart: 11, of which 9 were waited for; matrix products, arithmetic and copies ran while one was open for 16% of the time, Pallas kernels for 0%

commit v1 on v0

--- a/solution.py
+++ b/solution.py
@@ -10,6 +10,29 @@
 BLK = 128
 NBR = 8
 BND = 8
+
+
+def cut_along(value, dim, peers):
+    shape = value.shape
+    tiles = value.reshape(*shape[:dim], peers, shape[dim] // peers, *shape[dim + 1 :])
+    return jnp.moveaxis(tiles, dim, 0)
+
+
+def in_order(tiles, dim):
+    tiles = jnp.moveaxis(tiles, 0, dim)
+    shape = tiles.shape
+    return tiles.reshape(*shape[:dim], shape[dim] * shape[dim + 1], *shape[dim + 2 :])
+
+
+def rotated_exchange(x, axis, split_dim, concat_dim):
+    devices, index = (lax.axis_size(axis), lax.axis_index(axis))
+    blocks = cut_along(x, split_dim, devices)
+    outs = [blocks[index]]
+    for hop in range(1, devices):
+        sent = blocks[(index + hop) % devices]
+        outs.append(lax.ppermute(sent, axis, [(i, (i + hop) % devices) for i in range(devices)]))
+    blocks = jnp.stack(outs)[(index - jnp.arange(devices)) % devices]
+    return in_order(blocks, concat_dim)
 
 
 def with_halo(cells, sides, width):
@@ -117,7 +140,7 @@
 
     key_heads, value_heads = (
         lax.all_to_all(all_slots(keys), "seq", split_axis=0, concat_axis=1, tiled=True),
-        lax.all_to_all(all_slots(values), "seq", split_axis=0, concat_axis=1, tiled=True),
+        rotated_exchange(all_slots(values), "seq", 0, 1),
     )
     paired = jnp.stack([key_heads[0], value_heads[0]])
     head_first = paired.reshape(2, region_rows, pair_heads, HD).transpose(0, 2, 1, 3)

time: 434 us -> 428 us (0.986)
  waiting for transfers between devices: 144 us -> 135 us
  starting transfers between devices: 35.2 us -> 39.8 us
    ppermute x0 -> x7, starting transfers between devices: none -> 9.54 us  [rotated_exchange(): lax.ppermute(sent, axis, [(i, (i + hop) % devices) for i in range(devices)])]
    all_to_all x1, waiting for transfers between devices: 6.82 us -> 0.01 us  [body(): lax.all_to_all(all_slots(keys), 'seq', split_axis=0, concat_axis=1, tiled...]
    all_to_all x1 -> x0, waiting for transfers between devices: 6.78 us -> none  [body(): lax.all_to_all(all_slots(values), 'seq', split_axis=0, concat_axis=1, til...]
    all_to_all x1 -> x0, starting transfers between devices: 5.2 us -> none  [body(): lax.all_to_all(all_slots(values), 'seq', split_axis=0, concat_axis=1, til...]
    ppermute x0 -> x7, waiting for transfers between devices: none -> 4.88 us  [rotated_exchange(): lax.ppermute(sent, axis, [(i, (i + hop) % devices) for i in range(devices)])]
    unnamed x35 -> x45, local copies, waits for them, and re-layouts: 9.73 us -> 9.78 us
  transfers between devices with their start and end apart: 11 -> 17, of which waited for: 9 -> 8; matrix products, arithmetic and copies ran while one was open for 16% -> 16% of each run, Pallas kernels for 0% -> 0%
where the time goes in v1:
time: 428 us; the launch traced here: 420 us
  local copies, waits for them, and re-layouts  174 us (41%)
  waiting for transfers between devices  135 us (32%)
  other arithmetic  48.1 us (11%)
  starting transfers between devices  39.8 us (9%)
  matrix products  21.1 us (5%)
    ppermute x2, waiting for transfers between devices, with_halo(): lax.ppermute(tail, axis, [(i, (i + 1) % count) for i in range(count)])  54.1 us
    ppermute x2, waiting for transfers between devices, with_halo(): lax.ppermute(head, axis, [((i + 1) % count, i) for i in range(count)])  42.3 us
    all_to_all x1, waiting for transfers between devices, body(): lax.all_to_all(inner.reshape(2, seq_count, galaxies, pair_width), 'seq',...  24.6 us
    reshape x2, local copies, waits for them, and re-layouts, attend_group(): key_part.reshape(heads, group_size * neighbours, block_len, depth)  21.1 us
    reshape x2, local copies, waits for them, and re-layouts, attend_group(): value_part.reshape(heads, group_size * neighbours, block_len, depth)  20.8 us
    scatter-add x1, other arithmetic, attend_group(): value_acc.at[:, flat_ids]  13.6 us
    scatter-add x1, other arithmetic, attend_group(): key_acc.at[:, flat_ids]  13.4 us
    slice x2, local copies, waits for them, and re-layouts, body(): rim_out = accum[:, :, region_rows:].reshape(2, pair_heads, rim_rows, 2 * HD)  11.6 us
  transfers between devices with their start and end apart: 17, of which 8 were waited for; matrix products, arithmetic and copies ran while one was open for 16% of the time, Pallas kernels for 0%

profile of v1, /device:TPU:0, one launch (start us, length us, event | category | flops | bytes accessed | tf_op | source)
XLA Modules:
  0.0 420.2 jit_solution(555018767856405622)
XLA Ops:
  2.6 2.5 collective-permute-start.1
  5.2 2.4 collective-permute-start.2
  10.4 3.9 all-to-all-start
  16.1 3.0 collective-permute-start.5
  19.6 4.9 %collective-permute-done.5 = bf16[1,128,256]{2,1,0:T(8,128)(2,1)S(1)} collective-permute-done((bf16[1,128,256]{2,1,0:T(8,128)(2,1)S(1)}, bf16[1,128,256]{2,1,0:T(8,128)(2,1)S(1)}, u32[]{:S(2)}, u32[]{:S(2)}) %collective-permute-start.5) | collective-permute-done | bytes 65568 | tf_op jit(solution)/shard_map/ppermute | solution.py:33
  25.7 3.4 all-to-all-start.3
  32.6 1.5 pad_maximum_fusion.1
  34.1 4.8 %copy.177 = bf16[2,4,16,128,64]{4,3,2,1,0:T(8,128)(2,1)} copy(bf16[2,4,16,128,64]{3,4,1,0,2:T(8,128)(2,1)} %pad_maximum_fusion.1) | data formatting | bytes 4194304 | tf_op jit(solution)/shard_map/concatenate | solution.py:153
  38.9 5.0 %reshape.468 = bf16[2,4,1024,128]{3,2,1,0:T(8,128)(2,1)S(1)} reshape(bf16[2,4,16,128,64]{4,3,2,1,0:T(8,128)(2,1)} %copy.177) | data formatting | bytes 4194304 | tf_op jit(solution)/shard_map/reshape | solution.py:155
  44.0 1.5 fusion.68
  45.5 3.6 collective-permute-start.8
  53.0 4.3 %all-to-all-start.1 = ((bf16[8,64,256]{2,1,0:T(8,128)(2,1)}), bf16[8,64,256]{2,1,0:T(8,128)(2,1)S(1)}, u32[]{:S(2)}, u32[]{:S(2)}) async-start(bf16[8,64,256]{2,1,0:T(8,128)(2,1)} %bitcast.42), calls=%async_computation.1 | async-start | bytes 524288 | tf_op jit(solution)/shard_map/all_to_all | solution.py:133
  59.6 4.6 %all-to-all-done.1 = bf16[8,64,256]{2,1,0:T(8,128)(2,1)S(1)} async-done(((bf16[8,64,256]{2,1,0:T(8,128)(2,1)}), bf16[8,64,256]{2,1,0:T(8,128)(2,1)S(1)}, u32[]{:S(2)}, u32[]{:S(2)}) %all-to-all-start.1) | async-done | bytes 262176 | tf_op jit(solution)/shard_map/all_to_all | solution.py:133
  65.3 7.7 %collective-permute-done.8 = bf16[2,4,512,128]{3,2,1,0:T(8,128)(2,1)S(1)} collective-permute-done((bf16[2,4,512,128]{3,2,1,0:T(8,128)(2,1)}, bf16[2,4,512,128]{3,2,1,0:T(8,128)(2,1)S(1)}, u32[]{:S(2)}, u32[]{:S(2)}) %collective-permute-start.8) | collective-permute-done | bytes 1048608 | tf_op jit(solution)/shard_map/ppermute | solution.py:47
  73.8 1.6 copy.179
  75.4 20.4 %collective-permute-done.7 = bf16[2,4,512,128]{3,2,1,0:T(8,128)(2,1)} collective-permute-done((bf16[2,4,512,128]{3,2,1,0:T(8,128)(2,1)}, bf16[2,4,512,128]{3,2,1,0:T(8,128)(2,1)}, u32[]{:S(2)}, u32[]{:S(2)}) %collective-permute-start.7) | collective-permute-done | bytes 1048608 | tf_op jit(solution)/shard_map/ppermute | solution.py:45
  95.8 2.7 reshape.469
  98.5 1.6 copy.178
  100.2 1.7 pad_maximum_fusion
  102.8 3.1 gather_fusion.8
  106.7 3.1 gather_fusion.9
  109.7 6.7 %fusion.11 = f32[8,4,1024,64]{2,3,1,0:T(8,128)} fusion(bf16[8,8,4,8,8,128]{5,4,3,2,1,0:T(8,128)(2,1)} %bitcast.243, bf16[1,8,64,4,64]{4,3,2,1,0:T(4,128)(2,1)S(1)} %copy-done.4), kind=kOutput, calls=%fused_computation.28 | convolution fusion | flops 268435456 | bytes 12845056 | tf_op jit(solution)/shard_map/while/body/eval_jaxpr/bhqe,hbke->bhqk/dot_general | solution.py:73
  116.4 8.4 %fusion.70 = (f32[8,4,64]{2,1,0:T(4,128)S(1)}, f32[8,4,64,1024]{3,2,1,0:T(8,128)S(1)}) fusion(f32[8,4,1024,64]{2,3,1,0:T(8,128)} %fusion.11, pred[8,1024]{1,0:T(8,128)(4,1)S(1)} %fusion.50), kind=kOutput, calls=%fused_computation.137 | output fusion | flops 12583935 | bytes 16793600 | tf_op jit(solution)/shard_map/while/body/eval_jaxpr/sub | solution.py:78
  127.1 2.0 multiply_reduce_fusion
  129.2 4.5 %fusion.13 = f32[4,8,1024,64]{2,3,1,0:T(8,128)} fusion(bf16[8,4,64,1024]{3,2,1,0:T(8,128)(2,1)S(1)} %divide_convert_fusion, bf16[8,4,64,64]{2,3,1,0:T(8,128)(2,1)S(1)} %get-tuple-element.35), kind=kOutput, calls=%fused_computation.30 | convolution fusion | flops 268435456 | bytes 12845056 | tf_op jit(solution)/shard_map/while/body/eval_jaxpr/bhqk,bhqe->hbke/dot_general | solution.py:99
  133.7 1.9 multiply_convert_fusion
  135.6 2.0 copy-done.3
  137.5 1.3 broadcast_multiply_fusion
  138.8 8.1 %copy.199 = f32[4,8,1024,64]{2,1,3,0:T(8,128)} copy(f32[4,8,1024,64]{2,3,1,0:T(8,128)S(1)} %broadcast_multiply_fusion) | data formatting | bytes 16777216 | tf_op jit(solution)/shard_map/while/body/eval_jaxpr/mul | solution.py:97
  147.0 9.6 %reshape.576 = f32[4,64,128,64]{2,1,3,0:T(8,128)} reshape(f32[4,8,1024,64]{2,1,3,0:T(8,128)} %copy.199) | data formatting | bytes 16777216 | tf_op jit(solution)/shard_map/while/body/eval_jaxpr/reshape | solution.py:104
  156.6 11.5 %copy.200 = f32[64,4,128,64]{2,3,1,0:T(8,128)} copy(f32[64,4,128,64]{2,0,3,1:T(8,128)} %bitcast.247) | data formatting | bytes 16777216 | tf_op jit(solution)/shard_map/while/body/eval_jaxpr/reshape | solution.py:104
  168.5 13.4 %scatter_fusion = f32[4,24,128,64]{2,3,1,0:T(8,128)S(1)} fusion(f32[4,24,128,64]{2,3,1,0:T(8,128)S(1)} %broadcast.338.clone, s32[64]{0:T(128)S(1)} %reshape.527, f32[64,4,128,64]{2,3,1,0:T(8,128)} %copy.200), kind=kCustom, calls=%fused_computation.10 | custom fusion | flops 2097152 | bytes 25166080 | tf_op jit(solution)/shard_map/while/body/eval_jaxpr/scatter-add | solution.py:103
  181.8 3.5 copy.201
  185.4 3.0 stack.51
  188.4 1.8 constant_dynamic-update-slice_fusion.1
  190.2 11.5 %copy.204 = f32[4,8,1024,64]{2,1,3,0:T(8,128)} copy(f32[4,8,1024,64]{2,3,1,0:T(8,128)} %fusion.13) | data formatting | bytes 16777216 | tf_op jit(solution)/shard_map/while/body/eval_jaxpr/bhqk,bhqe->hbke/dot_general | solution.py:99
  201.7 9.3 %reshape.584 = f32[4,64,128,64]{2,1,3,0:T(8,128)} reshape(f32[4,8,1024,64]{2,1,3,0:T(8,128)} %copy.204) | data formatting | bytes 16777216 | tf_op jit(solution)/shard_map/while/body/eval_jaxpr/reshape | solution.py:107
  211.0 11.5 %copy.205 = f32[64,4,128,64]{2,3,1,0:T(8,128)} copy(f32[64,4,128,64]{2,0,3,1:T(8,128)} %bitcast.248) | data formatting | bytes 16777216 | tf_op jit(solution)/shard_map/while/body/eval_jaxpr/reshape | solution.py:107
  222.8 13.6 %scatter_fusion.1 = f32[4,24,128,64]{2,3,1,0:T(8,128)S(1)} fusion(f32[4,24,128,64]{2,3,1,0:T(8,128)S(1)} %broadcast.338.clone.1, s32[64]{0:T(128)S(1)} %reshape.527, f32[64,4,128,64]{2,3,1,0:T(8,128)} %copy.205), kind=kCustom, calls=%fused_computation.11 | custom fusion | flops 2097152 | bytes 25166080 | tf_op jit(solution)/shard_map/while/body/eval_jaxpr/scatter-add | solution.py:106
  236.4 3.4 copy.206
  239.9 2.8 stack.52
  242.7 1.9 constant_dynamic-update-slice_fusion
  244.6 4.7 %slice.79 = f32[2,4,2048,64]{2,3,1,0:T(8,128)} slice(f32[2,4,3072,64]{2,3,1,0:T(8,128)} %constant_dynamic-update-slice_fusion), slice={[0:2], [0:4], [1024:3072], [0:64]} | slice | bytes 8388608 | tf_op jit(solution)/shard_map/slice | solution.py:216
  249.2 7.0 %copy.207 = f32[2,4,2048,64]{3,2,1,0:T(8,128)} copy(f32[2,4,2048,64]{2,3,1,0:T(8,128)} %slice.79) | data formatting | bytes 8388608 | tf_op jit(solution)/shard_map/slice | solution.py:216
  256.2 7.2 %reshape.488 = f32[2,4,1024,128]{3,2,1,0:T(8,128)} reshape(f32[2,4,2048,64]{3,2,1,0:T(8,128)} %copy.207) | data formatting | bytes 8388608 | tf_op jit(solution)/shard_map/reshape | solution.py:216
  263.4 4.8 %fusion.66 = (f32[2,4,512,128]{3,2,1,0:T(8,128)}, f32[2,4,512,128]{3,2,1,0:T(8,128)}) fusion(f32[2,4,1024,128]{3,2,1,0:T(8,128)} %reshape.488), kind=kLoop, calls=%fused_computation.133 | loop fusion | bytes 8388608 | tf_op jit(solution)/shard_map/slice | solution.py:41
  268.2 1.4 collective-permute-start.9
  269.6 2.5 collective-permute-start.10
  273.0 4.1 all-to-all-start.2
  277.1 4.7 %fusion.40 = bf16[1,8,64,4,64]{4,2,3,1,0:T(8,128)(2,1)S(1)} fusion(bf16[8,4,64,1024]{3,2,1,0:T(8,128)(2,1)} %copy-done.3, bf16[8,8,4,8,8,128]{5,4,3,2,1,0:T(8,128)(2,1)} %bitcast.244), kind=kOutput, calls=%fused_computation.52 | convolution fusion | flops 268697600 | bytes 8650752 | tf_op jit(solution)/shard_map/while/body/eval_jaxpr/bhqk,hbke->bhqe/dot_general | solution.py:93
  283.2 1.9 copy_bitcast_fusion.1
  285.1 33.7 %collective-permute-done.9 = f32[2,4,512,128]{3,2,1,0:T(8,128)} collective-permute-done((f32[2,4,512,128]{3,2,1,0:T(8,128)}, f32[2,4,512,128]{3,2,1,0:T(8,128)}, u32[]{:S(2)}, u32[]{:S(2)}) %collective-permute-start.9) | collective-permute-done | bytes 2097184 | tf_op jit(solution)/shard_map/ppermute | solution.py:45
  318.9 4.3 %reshape.592 = f32[2,4,8,128,64]{4,3,2,1,0:T(8,128)} reshape(f32[2,4,512,128]{3,2,1,0:T(8,128)} %collective-permute-done.9) | data formatting | bytes 4194304 | tf_op jit(solution)/shard_map/reshape | solution.py:218
  323.2 3.9 copy.209
  327.1 34.6 %collective-permute-done.10 = f32[2,4,512,128]{3,2,1,0:T(8,128)} collective-permute-done((f32[2,4,512,128]{3,2,1,0:T(8,128)}, f32[2,4,512,128]{3,2,1,0:T(8,128)}, u32[]{:S(2)}, u32[]{:S(2)}) %collective-permute-start.10) | collective-permute-done | bytes 2097184 | tf_op jit(solution)/shard_map/ppermute | solution.py:47
  361.7 4.3 %reshape.600 = f32[2,4,8,128,64]{4,3,2,1,0:T(8,128)} reshape(f32[2,4,512,128]{3,2,1,0:T(8,128)} %collective-permute-done.10) | data formatting | bytes 4194304 | tf_op jit(solution)/shard_map/reshape | solution.py:219
  366.0 3.8 copy.210
  369.9 3.5 scatter_fusion.2
  373.3 3.5 scatter_fusion.3
  376.8 3.5 all-to-all-start.4
  381.1 1.7 copy.212
  382.8 4.4 %all-to-all-done.4 = bf16[8,64,256]{2,1,0:T(8,128)(2,1)S(1)} async-done(((bf16[8,64,256]{2,1,0:T(8,128)(2,1)}), bf16[8,64,256]{2,1,0:T(8,128)(2,1)S(1)}, u32[]{:S(2)}, u32[]{:S(2)}) %all-to-all-start.4) | async-done | bytes 262176 | tf_op jit(solution)/shard_map/all_to_all | solution.py:240
  387.2 3.6 all-to-all-start.5
  392.8 24.6 %all-to-all-done.5 = f32[2,8,128,256]{2,3,0,1:T(8,128)S(1)} async-done(((f32[2,8,128,256]{2,3,0,1:T(8,128)}), f32[2,8,128,256]{2,3,0,1:T(8,128)S(1)}, u32[]{:S(2)}, u32[]{:S(2)}) %all-to-all-start.5) | async-done | bytes 2097184 | tf_op jit(solution)/shard_map/all_to_all | solution.py:227
  (124 shorter events, 31.8 us)
Async XLA Ops:
  0.6 14.7 %copy-start = (s32[1,8,8]{2,1,0:T(8,128)S(1)}, s32[1,8,8]{2,1,0:T(8,128)}, u32[]{:S(2)}) copy-start(s32[1,8,8]{2,1,0:T(8,128)} %param.11) | copy-start | bytes 772
  0.6 13.7 %copy-start.8 = (bf16[128,1024]{1,0:T(8,128)(2,1)S(1)}, bf16[128,1024]{1,0:T(8,128)(2,1)}, u32[]{:S(2)}) copy-start(bf16[128,1024]{1,0:T(8,128)(2,1)} %param.10) | copy-start | bytes 786436
  0.7 14.6 %copy-start.14 = (s32[4,2,8]{2,1,0:T(2,128)S(1)}, s32[4,2,8]{2,1,0:T(2,128)}, u32[]{:S(2)}) copy-start(s32[4,2,8]{2,1,0:T(2,128)} %param.13) | copy-start | bytes 772
  0.7 15.4 %copy-start.13 = (s32[4,8]{1,0:T(4,128)S(1)}, s32[4,8]{1,0:T(4,128)}, u32[]{:S(2)}) copy-start(s32[4,8]{1,0:T(4,128)} %param.12) | copy-start | bytes 388
  2.1 14.0 %collective-permute-start = (bf16[1,128,256]{2,1,0:T(8,128)(2,1)S(1)}, bf16[1,128,256]{2,1,0:T(8,128)(2,1)S(1)}, u32[]{:S(2)}, u32[]{:S(2)}) collective-permute-start(bf16[1,128,256]{2,1,0:T(8,128)(2,1)S(1)} %get-tuple-element.65), channel_id=1, source_target_pairs={{0,1},{1,2},{2,3},{3,4},{4,5},{5,6},{6,7},{7,0},{8,9},{9,10},{10,1... | collective-permute-start | bytes 196616 | tf_op jit(solution)/shard_map/ppermute | solution.py:33
  2.6 16.4 %collective-permute-start.1 = (bf16[1,128,256]{2,1,0:T(8,128)(2,1)S(1)}, bf16[1,128,256]{2,1,0:T(8,128)(2,1)S(1)}, u32[]{:S(2)}, u32[]{:S(2)}) collective-permute-start(bf16[1,128,256]{2,1,0:T(8,128)(2,1)S(1)} %get-tuple-element.64), channel_id=1, source_target_pairs={{0,2},{1,3},{2,4},{3,5},{4,6},{5,7},{6,0},{7,1},{8,10},{9,11},{10,... | collective-permute-start | bytes 196616 | tf_op jit(solution)/shard_map/ppermute | solution.py:33
  5.2 14.4 %collective-permute-start.2 = (bf16[1,128,256]{2,1,0:T(8,128)(2,1)S(1)}, bf16[1,128,256]{2,1,0:T(8,128)(2,1)S(1)}, u32[]{:S(2)}, u32[]{:S(2)}) collective-permute-start(bf16[1,128,256]{2,1,0:T(8,128)(2,1)S(1)} %get-tuple-element.63), channel_id=1, source_target_pairs={{0,3},{1,4},{2,5},{3,6},{4,7},{5,0},{6,1},{7,2},{8,11},{9,12},{10,... | collective-permute-start | bytes 196616 | tf_op jit(solution)/shard_map/ppermute | solution.py:33
  7.5 12.0 %collective-permute-start.3 = (bf16[1,128,256]{2,1,0:T(8,128)(2,1)S(1)}, bf16[1,128,256]{2,1,0:T(8,128)(2,1)S(1)}, u32[]{:S(2)}, u32[]{:S(2)}) collective-permute-start(bf16[1,128,256]{2,1,0:T(8,128)(2,1)S(1)} %get-tuple-element.62), channel_id=1, source_target_pairs={{0,4},{1,5},{2,6},{3,7},{4,0},{5,1},{6,2},{7,3},{8,12},{9,13},{10,... | collective-permute-start | bytes 196616 | tf_op jit(solution)/shard_map/ppermute | solution.py:33
  8.1 11.6 %collective-permute-start.4 = (bf16[1,128,256]{2,1,0:T(8,128)(2,1)S(1)}, bf16[1,128,256]{2,1,0:T(8,128)(2,1)S(1)}, u32[]{:S(2)}, u32[]{:S(2)}) collective-permute-start(bf16[1,128,256]{2,1,0:T(8,128)(2,1)S(1)} %get-tuple-element.61), channel_id=1, source_target_pairs={{0,5},{1,6},{2,7},{3,0},{4,1},{5,2},{6,3},{7,4},{8,13},{9,14},{10,... | collective-permute-start | bytes 196616 | tf_op jit(solution)/shard_map/ppermute | solution.py:33
  10.4 15.2 %all-to-all-start = ((bf16[8,128,256]{1,2,0:T(8,128)(2,1)}), bf16[8,128,256]{1,2,0:T(8,128)(2,1)S(1)}, u32[]{:S(2)}, u32[]{:S(2)}) async-start(bf16[8,128,256]{1,2,0:T(8,128)(2,1)} %bitcast.13), calls=%async_computation | async-start | bytes 1048576 | tf_op jit(solution)/shard_map/all_to_all | solution.py:142
  15.3 0.7 copy-start.9
  15.3 0.7 copy-start.11
  16.1 8.4 %collective-permute-start.5 = (bf16[1,128,256]{2,1,0:T(8,128)(2,1)S(1)}, bf16[1,128,256]{2,1,0:T(8,128)(2,1)S(1)}, u32[]{:S(2)}, u32[]{:S(2)}) collective-permute-start(bf16[1,128,256]{2,1,0:T(8,128)(2,1)S(1)} %get-tuple-element.60), channel_id=1, source_target_pairs={{0,6},{1,7},{2,0},{3,1},{4,2},{5,3},{6,4},{7,5},{8,14},{9,15},{10,... | collective-permute-start | bytes 196616 | tf_op jit(solution)/shard_map/ppermute | solution.py:33
  19.1 5.4 %collective-permute-start.6 = (bf16[1,128,256]{2,1,0:T(8,128)(2,1)S(1)}, bf16[1,128,256]{2,1,0:T(8,128)(2,1)S(1)}, u32[]{:S(2)}, u32[]{:S(2)}) collective-permute-start(bf16[1,128,256]{2,1,0:T(8,128)(2,1)S(1)} %get-tuple-element.59), channel_id=1, source_target_pairs={{0,7},{1,0},{2,1},{3,2},{4,3},{5,4},{6,5},{7,6},{8,15},{9,8},{10,9... | collective-permute-start | bytes 196616 | tf_op jit(solution)/shard_map/ppermute | solution.py:33
  25.7 27.3 %all-to-all-start.3 = ((bf16[8,64,256]{2,1,0:T(8,128)(2,1)}), bf16[8,64,256]{2,1,0:T(8,128)(2,1)S(1)}, u32[]{:S(2)}, u32[]{:S(2)}) async-start(bf16[8,64,256]{2,1,0:T(8,128)(2,1)} %bitcast.54), calls=%async_computation.3 | async-start | bytes 524288 | tf_op jit(solution)/shard_map/all_to_all | solution.py:134
  45.5 27.5 %collective-permute-start.8 = (bf16[2,4,512,128]{3,2,1,0:T(8,128)(2,1)}, bf16[2,4,512,128]{3,2,1,0:T(8,128)(2,1)S(1)}, u32[]{:S(2)}, u32[]{:S(2)}) collective-permute-start(bf16[2,4,512,128]{3,2,1,0:T(8,128)(2,1)} %get-tuple-element.54), channel_id=1, source_target_pairs={{8,0},{16,8},{24,16},{0,24},{9,1},{17,9},{25,17},{1,25},{10,2},{18... | collective-permute-start | bytes 3145736 | tf_op jit(solution)/shard_map/ppermute | solution.py:47
  49.1 46.7 %collective-permute-start.7 = (bf16[2,4,512,128]{3,2,1,0:T(8,128)(2,1)}, bf16[2,4,512,128]{3,2,1,0:T(8,128)(2,1)}, u32[]{:S(2)}, u32[]{:S(2)}) collective-permute-start(bf16[2,4,512,128]{3,2,1,0:T(8,128)(2,1)} %get-tuple-element.53), channel_id=1, source_target_pairs={{0,8},{8,16},{16,24},{24,0},{1,9},{9,17},{17,25},{25,1},{2,10},{10... | collective-permute-start | bytes 3145736 | tf_op jit(solution)/shard_map/ppermute | solution.py:45
  53.0 11.2 %all-to-all-start.1 = ((bf16[8,64,256]{2,1,0:T(8,128)(2,1)}), bf16[8,64,256]{2,1,0:T(8,128)(2,1)S(1)}, u32[]{:S(2)}, u32[]{:S(2)}) async-start(bf16[8,64,256]{2,1,0:T(8,128)(2,1)} %bitcast.42), calls=%async_computation.1 | async-start | bytes 524288 | tf_op jit(solution)/shard_map/all_to_all | solution.py:133
  73.8 26.4 %copy-start.5 = (bf16[2,4,1024,64]{2,3,1,0:T(8,128)(2,1)S(1)}, bf16[2,4,1024,64]{2,3,1,0:T(8,128)(2,1)}, u32[]{:S(2)}) copy-start(bf16[2,4,1024,64]{2,3,1,0:T(8,128)(2,1)} %get-tuple-element.55) | copy-start | bytes 3145732
  106.6 3.1 copy-start.4
  124.8 2.2 copy-start.2
  124.8 2.3 copy-start.7
  135.5 2.0 copy-start.3
  263.4 8.6 %copy-start.6 = (bf16[8,4,64,64]{2,3,1,0:T(8,128)(2,1)S(1)}, bf16[8,4,64,64]{2,3,1,0:T(8,128)(2,1)}, u32[]{:S(2)}) copy-start(bf16[8,4,64,64]{2,3,1,0:T(8,128)(2,1)} %get-tuple-element.76) | copy-start | bytes 786436
  268.2 50.6 %collective-permute-start.9 = (f32[2,4,512,128]{3,2,1,0:T(8,128)}, f32[2,4,512,128]{3,2,1,0:T(8,128)}, u32[]{:S(2)}, u32[]{:S(2)}) collective-permute-start(f32[2,4,512,128]{3,2,1,0:T(8,128)} %get-tuple-element.37), channel_id=1, source_target_pairs={{0,8},{8,16},{16,24},{24,0},{1,9},{9,17},{17,25},{25,1},{2,10},{10... | collective-permute-start | bytes 6291464 | tf_op jit(solution)/shard_map/ppermute | solution.py:45
  269.6 92.1 %collective-permute-start.10 = (f32[2,4,512,128]{3,2,1,0:T(8,128)}, f32[2,4,512,128]{3,2,1,0:T(8,128)}, u32[]{:S(2)}, u32[]{:S(2)}) collective-permute-start(f32[2,4,512,128]{3,2,1,0:T(8,128)} %get-tuple-element.36), channel_id=1, source_target_pairs={{8,0},{16,8},{24,16},{0,24},{9,1},{17,9},{25,17},{1,25},{10,2},{18... | collective-permute-start | bytes 6291464 | tf_op jit(solution)/shard_map/ppermute | solution.py:47
  273.0 103.9 %all-to-all-start.2 = ((bf16[8,64,256]{2,1,0:T(8,128)(2,1)}), bf16[8,64,256]{2,1,0:T(8,128)(2,1)S(1)}, u32[]{:S(2)}, u32[]{:S(2)}) async-start(bf16[8,64,256]{2,1,0:T(8,128)(2,1)} %copy.188), calls=%async_computation.2 | async-start | bytes 524288 | tf_op jit(solution)/shard_map/all_to_all | solution.py:239
  366.0 3.8 copy-start.12
  369.9 3.5 copy-start.10
  376.8 10.4 %all-to-all-start.4 = ((bf16[8,64,256]{2,1,0:T(8,128)(2,1)}), bf16[8,64,256]{2,1,0:T(8,128)(2,1)S(1)}, u32[]{:S(2)}, u32[]{:S(2)}) async-start(bf16[8,64,256]{2,1,0:T(8,128)(2,1)} %reshape.482), calls=%async_computation.4 | async-start | bytes 524288 | tf_op jit(solution)/shard_map/all_to_all | solution.py:240
  387.2 30.2 %all-to-all-start.5 = ((f32[2,8,128,256]{2,3,0,1:T(8,128)}), f32[2,8,128,256]{2,3,0,1:T(8,128)S(1)}, u32[]{:S(2)}, u32[]{:S(2)}) async-start(f32[2,8,128,256]{2,3,0,1:T(8,128)} %copy.212), calls=%async_computation.5 | async-start | bytes 4194304 | tf_op jit(solution)/shard_map/all_to_all | solution.py:227
  391.1 28.8 %copy-start.1 = (s32[1,8,8]{2,1,0:T(8,128)S(1)}, s32[1,8,8]{2,1,0:T(8,128)}, u32[]{:S(2)}) copy-start(s32[1,8,8]{2,1,0:T(8,128)} %param.11) | copy-start | bytes 772
